TPU v7x, 512 devices: a whole 4x8x8 slice. The times are simulated.
512 devices in a mesh: lower: 16 (over y, core), upper: 8 (over z), depth: 4 (over x).
Axes of the slice: x: 4, y: 8, z: 8, core: 2. Of those that a mesh axis runs over, the one named last changes fastest.
Arguments:
- lower_vectors: bfloat16 [4, 32768, 2048], P('depth', 'lower', 'upper'), may hold values from -0.0234375 to 0.0234375
- upper_vectors: bfloat16 [4, 32768, 3072], P('depth', 'lower', 'upper'), may hold values from -6 to 6
- energy_lower: float32 [2048], P(('lower', 'depth')), may hold values from 0 to 0.5
- energy_upper: float32 [3072], P('upper'), may hold values from 1 to 2
- sym_lower: int32 [2048], P(('lower', 'depth')), may hold values from 0 to 3
- sym_upper: int32 [3072], P('upper'), may hold values from 0 to 3
- j_lower: int32 [2048], P(('lower', 'depth')), may hold values from 0 to 2
- j_upper: int32 [3072], P('upper'), may hold values from 0 to 2
Outputs:
- einstein: float32 [2048, 3072], P(('lower', 'depth'), 'upper')
All inputs are finite; a program needn't handle non-finite values.
Results may differ from a plain program's by a relative error of at most 0.0003.
Values may be sent and summed in bfloat16 or wider, within the bound.
A program may use at most 64 MiB of HBM per device.

v0:
```python
import jax
import jax.numpy as jnp
from jax import lax
from jax.sharding import PartitionSpec as P


def local(
    lower_vectors, upper_vectors, energy_lower, energy_upper, sym_lower, sym_upper, j_lower, j_upper
):
    lower_rows = lower_vectors[0]
    upper_rows = upper_vectors[0]
    partial_terms = lax.dot_general(
        lax.all_gather(lower_rows, "upper", axis=1, tiled=True),
        upper_rows,
        (((0,), (0,)), ((), ())),
        preferred_element_type=jnp.float32,
    )
    moments = lax.psum_scatter(partial_terms, ("lower", "depth"), scatter_dimension=0, tiled=True)
    parity = sym_lower % 2
    sym_rule = sym_upper[None, :] - sym_lower[:, None] == (1 - 2 * parity)[:, None]
    j_rule = jnp.abs(j_upper[None, :] - j_lower[:, None]) <= 1
    allowed = jnp.logical_and(sym_rule, j_rule)
    frequency = energy_upper[None, :] - energy_lower[:, None]
    weight_upper = (2 * j_upper + 1).astype(jnp.float32)
    value = frequency * frequency * frequency * (moments * moments) / weight_upper[None, :]
    return jnp.where(allowed, value, jnp.zeros_like(value))


def solution(mesh):
    return jax.shard_map(
        local,
        mesh=mesh,
        in_specs=(
            P("depth", "lower", "upper"),
            P("depth", "lower", "upper"),
            P(("lower", "depth")),
            P("upper"),
            P(("lower", "depth")),
            P("upper"),
            P(("lower", "depth")),
            P("upper"),
        ),
        out_specs=P(("lower", "depth"), "upper"),
        check_vma=False,
    )
```

profile of v0, /device:TPU:16, one launch (start us, length us, event | category | flops | bytes accessed | tf_op | source)
XLA Modules:
  0.0 283.6 jit_solution(9405413848341315890)
XLA Ops:
  6.5 0.0 copy-start
  6.5 0.0 all-gather.3.cloned.1.call-start
  6.5 0.7 all-gather.3.cloned.1.call-update
  7.3 0.0 reduce-scatter.2.cloned.1.call-start
  7.3 110.6 %all-gather.3.cloned.1.call-done = bf16[1,2048,2048]{2,1,0:T(8,128)(2,1)} async-done(((bf16[1,2048,256]{2,1,0:T(8,128)(2,1)}), bf16[1,2048,2048]{2,1,0:T(8,128)(2,1)}) %all-gather.3.cloned.1.call-update) | async-done | bytes 8388624 | tf_op jit(solution)/shard_map/all_gather | solution.py:13
  117.9 0.0 copy-done
  117.9 8.7 %fusion = f32[2048,384]{1,0:T(8,128)} fusion(bf16[1,2048,2048]{2,1,0:T(8,128)(2,1)} %all-gather.3.cloned.1.call-done, bf16[1,2048,384]{2,1,0:T(8,128)(2,1)S(1)} %copy-done), kind=kOutput, calls=%fused_computation | convolution fusion | flops 3221225472 | bytes 13107200 | tf_op jit(solution)/shard_map/dot_general | solution.py:12
  126.6 0.0 copy-start.6
  126.6 0.0 copy-start.1
  126.6 0.0 copy-start.2
  126.6 0.0 copy-start.3
  126.7 0.0 copy-start.4
  126.7 0.0 copy-start.5
  126.7 0.0 reduce-scatter.2.cloned.1.call-update
  126.7 0.6 copy-done.6
  127.3 0.0 copy-done.1
  127.3 147.9 %reduce-scatter.2.cloned.1.call-done = f32[32,384]{1,0:T(8,128)} async-done(((f32[2048,384]{1,0:T(8,128)}), f32[32,384]{1,0:T(8,128)}) %reduce-scatter.2.cloned.1.call-update) | async-done | bytes 49168 | tf_op jit(solution)/shard_map/reduce_scatter | solution.py:18
  275.2 0.0 copy-done.2
  275.2 0.0 copy-done.3
  275.2 0.0 copy-done.4
  275.2 0.0 copy-done.5
  275.2 1.5 fusion.5
  (2 shorter events, 0.0 us)
Async XLA Ops:
  6.5 111.4 %copy-start = (bf16[1,2048,384]{2,1,0:T(8,128)(2,1)S(1)}, bf16[1,2048,384]{2,1,0:T(8,128)(2,1)}, u32[]{:S(2)}) copy-start(bf16[1,2048,384]{2,1,0:T(8,128)(2,1)} %param.9) | copy-start | bytes 4718596
  6.5 111.4 %all-gather.3.cloned.1.call-start = ((), (), s32[]{:S(2)}) async-start(), calls=%async_computation.2 | async-start | bytes 9437184 | tf_op jit(solution)/shard_map/all_gather | solution.py:13
  7.3 268.0 %reduce-scatter.2.cloned.1.call-start = ((), (), s32[]{:S(2)}) async-start(), calls=%async_computation.1 | async-start | bytes 3194880 | tf_op jit(solution)/shard_map/reduce_scatter | solution.py:18
  126.6 0.7 copy-start.6
  126.6 0.7 copy-start.1
  126.6 148.6 %copy-start.2 = (f32[384]{0:T(512)S(1)}, f32[384]{0:T(512)}, u32[]{:S(2)}) copy-start(f32[384]{0:T(512)} %param.11) | copy-start | bytes 4612
  126.6 148.6 %copy-start.3 = (s32[384]{0:T(512)S(1)}, s32[384]{0:T(512)}, u32[]{:S(2)}) copy-start(s32[384]{0:T(512)} %param.13) | copy-start | bytes 4612
  126.7 148.6 %copy-start.4 = (f32[32]{0:T(128)S(1)}, f32[32]{0:T(128)}, u32[]{:S(2)}) copy-start(f32[32]{0:T(128)} %param.10) | copy-start | bytes 388
  126.7 148.6 %copy-start.5 = (s32[32]{0:T(128)S(1)}, s32[32]{0:T(128)}, u32[]{:S(2)}) copy-start(s32[32]{0:T(128)} %param.14) | copy-start | bytes 388
Sparse Core Ops, SparseCore 0:
  9.4 108.5 all-gather.2
  126.8 148.3 reduce-scatter.1
where the time goes:
time: 284 us
  waiting for transfers between devices  259 us (91%)
  between operations  13.4 us (5%)
  matrix products  8.69 us (3%)
    reduce_scatter x1, waiting for transfers between devices, local(): lax.psum_scatter(partial_terms, ('lower', 'depth'), scatter_dimension=0,...  148 us
    all_gather x1, waiting for transfers between devices, local(): lax.all_gather(lower_rows, 'upper', axis=1, tiled=True)  111 us
    dot_general x1, matrix products, local(): lax.dot_general(lax.all_gather(lower_rows, 'upper', axis=1, tiled=True),...  8.69 us
  transfers between devices with their start and end apart: 2, of which 2 were waited for; matrix products, arithmetic and copies ran while one was open for 0% of the time, Pallas kernels for 0%

commit v1 on v0

v1 whole, which is shorter than its diff:
```python
import functools

import jax
import jax.numpy as jnp
from jax import lax
from jax.experimental import pallas as pl
from jax.experimental.pallas import tpu as pltpu
from jax.sharding import PartitionSpec as P

MESH = pl.DeviceIdType.MESH
F32 = jnp.float32
PIECES = 4


def moments_kernel(
    lower_hbm, upper_hbm, out_ref,
    block, upper, acc, from_core, half, from_x, quarter, from_y,
    load_sem, ring_send, ring_recv, core_send, core_recv, x_send, x_recv, y_send, y_recv,
    *, n_y, n_z, n_x,
):
    li, z, x = lax.axis_index("lower"), lax.axis_index("upper"), lax.axis_index("depth")
    y, core = li // 2, lax.rem(li, 2)
    rows_all = block.shape[1]
    piece = rows_all // PIECES
    far = n_z // 2
    right, left = {"upper": lax.rem(z + 1, n_z)}, {"upper": lax.rem(z + n_z - 1, n_z)}
    sibling = {"lower": y * 2 + 1 - core}

    load_lower = pltpu.make_async_copy(lower_hbm, block.at[0], load_sem.at[0])
    load_upper = pltpu.make_async_copy(upper_hbm, upper, load_sem.at[1])
    load_lower.start()
    load_upper.start()

    barrier = pltpu.get_barrier_semaphore()
    for who in (right, left, sibling):
        pl.semaphore_signal(barrier, inc=1, device_id=who, device_id_type=MESH)
    for k in range(1, n_x):
        pl.semaphore_signal(barrier, inc=1, device_id={"depth": lax.rem(x + k, n_x)}, device_id_type=MESH)
    for k in range(1, n_y):
        pl.semaphore_signal(barrier, inc=1, device_id={"lower": lax.rem(y + k, n_y) * 2 + core}, device_id_type=MESH)
    pl.semaphore_wait(barrier, 3 + n_x - 1 + n_y - 1)

    def slot(way, d):
        if d == 0:
            return 0
        if d == far:
            return 2 * far - 1
        return d if way == 0 else far - 1 + d

    def hop(way, d, p):
        rows = pl.ds(pl.multiple_of(p * piece, piece), piece)
        to = slot(way, d)
        return pltpu.make_async_remote_copy(
            src_ref=block.at[slot(way, d - 1), rows],
            dst_ref=block.at[to, rows],
            send_sem=ring_send.at[to, p],
            recv_sem=ring_recv.at[to, p],
            device_id=right if way == 0 else left,
            device_id_type=MESH,
        )

    def goes(way, d, p):
        return d < far or (p < PIECES // 2) == (way == 0)

    load_lower.wait()
    for p in range(PIECES):
        for way in (0, 1):
            hop(way, 1, p).start()
    load_upper.wait()

    def product(b):
        return lax.dot_general(block[b], upper[...], (((0,), (0,)), ((), ())), preferred_element_type=F32)

    def core_copy(b):
        theirs = pl.ds(pl.multiple_of((1 - core) * half.shape[1], 8), half.shape[1])
        return pltpu.make_async_remote_copy(
            src_ref=acc.at[b, theirs], dst_ref=from_core.at[b],
            send_sem=core_send.at[b], recv_sem=core_recv.at[b], device_id=sibling, device_id_type=MESH,
        )

    def x_copy(b, k):
        to = lax.rem(x + k, n_x)
        n = quarter.shape[1]
        return pltpu.make_async_remote_copy(
            src_ref=half.at[b, pl.ds(pl.multiple_of(to * n, 8), n)], dst_ref=from_x.at[b, k - 1],
            send_sem=x_send.at[b, k - 1], recv_sem=x_recv.at[b, k - 1], device_id={"depth": to}, device_id_type=MESH,
        )

    def owner(b):
        if b == 0:
            return z
        if b < far:
            return lax.rem(z + n_z - b, n_z)
        if b < 2 * far - 1:
            return lax.rem(z + b - far + 1, n_z)
        return lax.rem(z + far, n_z)

    def y_copy(b, who):
        return pltpu.make_async_remote_copy(
            src_ref=quarter.at[b], dst_ref=from_y.at[y],
            send_sem=y_send.at[b], recv_sem=y_recv.at[y], device_id={"lower": who * 2 + core}, device_id_type=MESH,
        )

    def first(b):
        acc[b] = product(b)
        core_copy(b).start()

    def second(b):
        core_copy(b).wait_recv()
        mine = pl.ds(pl.multiple_of(core * half.shape[1], 8), half.shape[1])
        half[b] = acc[b, mine] + from_core[b]
        for k in range(1, n_x):
            x_copy(b, k).start()

    def third(b):
        n = quarter.shape[1]
        total = half[b, pl.ds(pl.multiple_of(x * n, 8), n)]
        for k in range(1, n_x):
            x_copy(b, k).wait_recv()
            total = total + from_x[b, k - 1]
        quarter[b] = total
        who = owner(b)

        @pl.when(who != y)
        def _():
            y_copy(b, who).start()

        @pl.when(who == y)
        def _():
            from_y[y] = quarter[b]

    groups = [[0]] + [[d, far - 1 + d] for d in range(1, far)] + [[2 * far - 1]]
    for s in range(len(groups) + 2):
        if 1 <= s < len(groups):
            for p in range(PIECES):
                for way in (0, 1):
                    if goes(way, s, p):
                        hop(way, s, p).wait_recv()
                        if s < far and goes(way, s + 1, p):
                            hop(way, s + 1, p).start()
        if s < len(groups):
            for b in groups[s]:
                first(b)
        if 1 <= s and s - 1 < len(groups):
            for b in groups[s - 1]:
                second(b)
        if 2 <= s:
            for b in groups[s - 2]:
                third(b)

    for k in range(1, n_y):
        peer = lax.rem(y + k, n_y)
        pltpu.make_async_remote_copy(
            src_ref=quarter.at[0], dst_ref=from_y.at[peer],
            send_sem=y_send.at[0], recv_sem=y_recv.at[peer], device_id={"lower": peer * 2 + core}, device_id_type=MESH,
        ).wait_recv()
    total = from_y[0]
    for k in range(1, n_y):
        total = total + from_y[k]
    out_ref[...] = total

    for d in range(1, far + 1):
        for p in range(PIECES):
            for way in (0, 1):
                if goes(way, d, p):
                    hop(way, d, p).wait_send()
    for b in range(2 * far):
        core_copy(b).wait_send()
        for k in range(1, n_x):
            x_copy(b, k).wait_send()
        who = owner(b)

        @pl.when(who != y)
        def _():
            y_copy(b, who).wait_send()


def local(
    lower_vectors, upper_vectors, energy_lower, energy_upper, sym_lower, sym_upper, j_lower, j_upper,
    *, n_y, n_z, n_x,
):
    rows, n_l = lower_vectors.shape[1:]
    n_u = upper_vectors.shape[2]
    n_out = n_l // (2 * n_x)
    vmem = pl.BlockSpec(memory_space=pltpu.VMEM)
    hbm = pl.BlockSpec(memory_space=pl.ANY)
    dma = pltpu.SemaphoreType.DMA
    moments = pl.pallas_call(
        functools.partial(moments_kernel, n_y=n_y, n_z=n_z, n_x=n_x),
        out_shape=jax.ShapeDtypeStruct((n_out, n_u), F32),
        in_specs=[hbm, hbm],
        out_specs=vmem,
        scratch_shapes=[
            pltpu.VMEM((n_z, rows, n_l), lower_vectors.dtype),
            pltpu.VMEM((rows, n_u), upper_vectors.dtype),
            pltpu.VMEM((n_z, n_l, n_u), F32),
            pltpu.VMEM((n_z, n_l // 2, n_u), F32),
            pltpu.VMEM((n_z, n_l // 2, n_u), F32),
            pltpu.VMEM((n_z, n_x - 1, n_out, n_u), F32),
            pltpu.VMEM((n_z, n_out, n_u), F32),
            pltpu.VMEM((n_y, n_out, n_u), F32),
            dma((2,)),
            dma((n_z, PIECES)), dma((n_z, PIECES)),
            dma((n_z,)), dma((n_z,)),
            dma((n_z, n_x - 1)), dma((n_z, n_x - 1)),
            dma((n_z,)), dma((n_y,)),
        ],
        compiler_params=pltpu.CompilerParams(
            collective_id=0, has_side_effects=True, vmem_limit_bytes=48 << 20
        ),
    )(lower_vectors[0], upper_vectors[0])
    parity = sym_lower % 2
    sym_rule = sym_upper[None, :] - sym_lower[:, None] == (1 - 2 * parity)[:, None]
    j_rule = jnp.abs(j_upper[None, :] - j_lower[:, None]) <= 1
    allowed = jnp.logical_and(sym_rule, j_rule)
    frequency = energy_upper[None, :] - energy_lower[:, None]
    weight_upper = (2 * j_upper + 1).astype(F32)
    value = frequency * frequency * frequency * (moments * moments) / weight_upper[None, :]
    return jnp.where(allowed, value, jnp.zeros_like(value))


def solution(mesh):
    sizes = dict(mesh.shape)
    return jax.shard_map(
        functools.partial(local, n_y=sizes["lower"] // 2, n_z=sizes["upper"], n_x=sizes["depth"]),
        mesh=mesh,
        in_specs=(
            P("depth", "lower", "upper"),
            P("depth", "lower", "upper"),
            P(("lower", "depth")),
            P("upper"),
            P(("lower", "depth")),
            P("upper"),
            P(("lower", "depth")),
            P("upper"),
        ),
        out_specs=P(("lower", "depth"), "upper"),
        check_vma=False,
    )
```

time: 284 us -> 115 us (0.40)
  the two profiles are of different devices: /device:TPU:16 before, /device:TPU:24 now
where the time goes in v1:
time: 115 us
  Pallas kernels  110 us (96%)
  local copies, waits for them, and re-layouts  2.66 us (2%)
  other arithmetic  2.12 us (2%)
    pallas_call x1, Pallas kernels, local(): pl.pallas_call(functools.partial(moments_kernel, n_y=n_y, n_z=n_z, n_x=n_...  110 us
    unnamed x16, local copies, waits for them, and re-layouts  2.66 us

profile of v1, /device:TPU:24, one launch (start us, length us, event | category | flops | bytes accessed | tf_op | source)
XLA Modules:
  0.0 114.8 jit_solution(5922024444479371080)
XLA Ops:
  0.0 0.0 copy-start.2
  0.0 0.0 copy-start.7
  0.0 0.0 copy-start.6
  0.0 0.0 copy-start.4
  0.0 0.0 copy-start.3
  0.0 0.0 copy-start.5
  0.0 0.7 fusion.5
  0.8 0.7 add_convert_fusion
  1.4 0.0 copy-start
  1.4 1.4 %copy-done = bf16[1,2048,384]{2,1,0:T(8,128)(2,1)S(1)} copy-done((bf16[1,2048,384]{2,1,0:T(8,128)(2,1)S(1)}, bf16[1,2048,384]{2,1,0:T(8,128)(2,1)}, u32[]{:S(2)}) %copy-start) | copy-done | bytes 1572888
  2.9 0.0 copy-start.1
  2.9 1.2 %copy-done.1 = bf16[1,2048,256]{2,1,0:T(8,128)(2,1)S(1)} copy-done((bf16[1,2048,256]{2,1,0:T(8,128)(2,1)S(1)}, bf16[1,2048,256]{2,1,0:T(8,128)(2,1)}, u32[]{:S(2)}) %copy-start.1) | copy-done | bytes 1048600
  4.1 109.9 %shard_map.82 = f32[32,384]{1,0:T(8,128)S(1)} custom-call(bf16[2048,256]{1,0:T(8,128)(2,1)S(1)} %bitcast.3, bf16[2048,384]{1,0:T(8,128)(2,1)S(1)} %bitcast.2), custom_call_target="tpu_custom_call" | custom-call | tf_op jit(solution)/shard_map/pallas_call | solution.py:188
  114.0 0.0 copy-done.2
  114.0 0.0 copy-done.7
  114.0 0.0 copy-done.6
  114.0 0.0 copy-done.4
  114.1 0.0 copy-done.3
  114.1 0.0 copy-done.5
  114.1 0.7 fusion.2
Async XLA Ops:
  0.0 114.0 %copy-start.2 = (s32[384]{0:T(512)S(1)}, s32[384]{0:T(512)}, u32[]{:S(2)}) copy-start(s32[384]{0:T(512)} %param.15) | copy-start | bytes 4612
  0.0 114.0 %copy-start.7 = (s32[32]{0:T(128)S(1)}, s32[32]{0:T(128)}, u32[]{:S(2)}) copy-start(s32[32]{0:T(128)} %param.12) | copy-start | bytes 388
  0.0 114.0 %copy-start.6 = (s32[32]{0:T(128)S(1)}, s32[32]{0:T(128)}, u32[]{:S(2)}) copy-start(s32[32]{0:T(128)} %param.14) | copy-start | bytes 388
  0.0 114.0 %copy-start.4 = (s32[384]{0:T(512)S(1)}, s32[384]{0:T(512)}, u32[]{:S(2)}) copy-start(s32[384]{0:T(512)} %param.13) | copy-start | bytes 4612
  0.0 114.0 %copy-start.3 = (f32[384]{0:T(512)S(1)}, f32[384]{0:T(512)}, u32[]{:S(2)}) copy-start(f32[384]{0:T(512)} %param.11) | copy-start | bytes 4612
  0.0 114.0 %copy-start.5 = (f32[32]{0:T(128)S(1)}, f32[32]{0:T(128)}, u32[]{:S(2)}) copy-start(f32[32]{0:T(128)} %param.10) | copy-start | bytes 388
  1.4 1.4 %copy-start = (bf16[1,2048,384]{2,1,0:T(8,128)(2,1)S(1)}, bf16[1,2048,384]{2,1,0:T(8,128)(2,1)}, u32[]{:S(2)}) copy-start(bf16[1,2048,384]{2,1,0:T(8,128)(2,1)} %param.9) | copy-start | bytes 4718596
  2.9 1.2 %copy-start.1 = (bf16[1,2048,256]{2,1,0:T(8,128)(2,1)S(1)}, bf16[1,2048,256]{2,1,0:T(8,128)(2,1)}, u32[]{:S(2)}) copy-start(bf16[1,2048,256]{2,1,0:T(8,128)(2,1)} %param.8) | copy-start | bytes 3145732

commit v2 on v0

v2 whole, which is shorter than its diff:
```python
import functools

import jax
import jax.numpy as jnp
from jax import lax
from jax.experimental import pallas as pl
from jax.experimental.pallas import tpu as pltpu
from jax.sharding import PartitionSpec as P

MESH = pl.DeviceIdType.MESH
F32 = jnp.float32
N_Z = 8
N_Y = 8
N_X = 4
SLICES = 4

E_AT = {1: 0, 2: 1, -1: 2, -2: 3, -3: 4, -4: 5, -5: 6}
M_AT = {1: 7, 2: 8, 3: 9, 4: 10, -1: 11, -2: 12, -3: 13}
PASS_L, NEAR_U, FAR_U, PASS_U = 14, 15, 16, 17
FLOWS = 18


def moments_kernel(
    lower_hbm, upper_hbm, out_ref,
    lower, upper, e_block, m_block, pass_l, pass_u, upper_e,
    acc, half, from_x1, second_x, from_x2, quarter, from_y, sums, from_z,
    load_sem, ring_send, ring_recv, core_send, core_recv, x1_send, x1_recv, x2_send, x2_recv, y_send, y_recv,
    z_send, z_recv,
):
    li, z, x = lax.axis_index("lower"), lax.axis_index("upper"), lax.axis_index("depth")
    y, core = li // 2, lax.rem(li, 2)
    depth = lower.shape[0] // SLICES
    n_l, n_u = lower.shape[1], upper.shape[1]
    wide = n_l // 2
    n_out = wide // N_X

    place = lax.rem(z + lax.rem(y, 2), N_Z)
    out = 2 * lax.rem(place, 2) - 1
    home_a = place // 4
    home_b = 2 + lax.rem(place + 6, N_Z) // 4
    end_a = 1 - lax.rem(place + 1, 4) // 2
    e_row = end_a * home_a + (1 - end_a) * home_b
    m_row = end_a * home_b + (1 - end_a) * home_a
    e_away = end_a * (1 - home_a) + (1 - end_a) * (5 - home_b)
    m_away = end_a * (5 - home_b) + (1 - end_a) * (1 - home_a)

    def plane(step):
        return {"upper": lax.rem(z + step + 2 * N_Z, N_Z)}

    outer, inner = plane(out), plane(-out)
    sibling = {"lower": y * 2 + 1 - core}
    flip, mirror = x + 1 - 2 * lax.rem(x, 2), 3 - x
    x1 = flip * (1 - core) + mirror * core
    x2 = mirror * (1 - core) + flip * core
    x3 = lax.rem(x + 2, N_X)

    load_lower = pltpu.make_async_copy(lower_hbm, lower, load_sem.at[0])
    load_upper = pltpu.make_async_copy(upper_hbm, upper, load_sem.at[1])
    load_upper.start()
    load_lower.start()

    barrier = pltpu.get_barrier_semaphore()
    partners = [plane(s) for s in (1, -1, 2, -2)] + [sibling, {"depth": flip}, {"depth": mirror}]
    partners += [{"lower": lax.rem(y + k, N_Y) * 2 + core} for k in range(1, N_Y)]
    for who in partners:
        pl.semaphore_signal(barrier, inc=1, device_id=who, device_id_type=MESH)
    pl.semaphore_wait(barrier, len(partners))

    def rows(k):
        return pl.ds(pl.multiple_of(k * depth, depth), depth)

    def states(p):
        return pl.ds(p * wide, wide)

    def e_piece(d, p):
        return lower.at[rows(e_row), states(p)] if d == 0 else e_block.at[E_AT[d], :, states(p)]

    def m_piece(d, p):
        return lower.at[rows(m_row), states(p)] if d == 0 else m_block.at[M_AT[d] - 7, :, states(p)]

    def ring(flow, p):
        part = depth // 2
        if flow == E_AT[1]:
            src, dst, who = lower.at[rows(e_away), states(p)], e_block.at[0, :, states(p)], outer
        elif flow == E_AT[2]:
            src, dst, who = pass_l.at[:, states(p)], e_block.at[1, :, states(p)], outer
        elif flow <= E_AT[-5]:
            src, dst, who = m_piece(flow - 2, p), e_block.at[flow, :, states(p)], inner
        elif flow <= M_AT[4]:
            src, dst, who = m_piece(7 - flow, p), m_block.at[flow - 7, :, states(p)], outer
        elif flow <= M_AT[-3]:
            src, dst, who = e_piece(flow - 11, p), m_block.at[flow - 7, :, states(p)], inner
        elif flow == PASS_L:
            src, dst, who = lower.at[rows(m_away), states(p)], pass_l.at[:, states(p)], inner
        elif flow == NEAR_U:
            src = upper.at[pl.ds(pl.multiple_of(e_away * depth + p * part, part), part)]
            dst, who = upper_e.at[pl.ds(p * part, part), pl.ds(n_u, n_u)], outer
        elif flow == FAR_U:
            src = pass_u.at[pl.ds(p * part, part)]
            dst, who = upper_e.at[pl.ds(p * part, part), pl.ds(2 * n_u, n_u)], outer
        else:
            src = upper.at[pl.ds(pl.multiple_of(m_away * depth + p * part, part), part)]
            dst, who = pass_u.at[pl.ds(p * part, part)], inner
        return pltpu.make_async_remote_copy(
            src_ref=src, dst_ref=dst, send_sem=ring_send.at[flow, p], recv_sem=ring_recv.at[flow, p],
            device_id=who, device_id_type=MESH,
        )

    def send(flow):
        for p in (0, 1):
            ring(flow, p).start()

    load_upper.wait()
    send(NEAR_U)
    send(PASS_U)
    load_lower.wait()
    send(PASS_L)
    send(M_AT[-1])
    send(E_AT[-1])
    upper_e[:, pl.ds(0, n_u)] = upper[rows(e_row), :]

    def core_copy(u):
        return pltpu.make_async_remote_copy(
            src_ref=acc.at[u, 1 - core], dst_ref=half.at[u],
            send_sem=core_send.at[u], recv_sem=core_recv.at[u], device_id=sibling, device_id_type=MESH,
        )

    def block(k):
        return pl.ds(pl.multiple_of(k * n_out, n_out), n_out)

    def x1_copy(u, k):
        return pltpu.make_async_remote_copy(
            src_ref=half.at[u, block(x1 if k == 0 else x3)], dst_ref=from_x1.at[u, k],
            send_sem=x1_send.at[u, k], recv_sem=x1_recv.at[u, k], device_id={"depth": x1}, device_id_type=MESH,
        )

    def x2_copy(u):
        return pltpu.make_async_remote_copy(
            src_ref=second_x.at[u], dst_ref=from_x2.at[u],
            send_sem=x2_send.at[u], recv_sem=x2_recv.at[u], device_id={"depth": x2}, device_id_type=MESH,
        )

    def y_copy(u, sem, slot, who):
        return pltpu.make_async_remote_copy(
            src_ref=quarter.at[u], dst_ref=from_y.at[slot],
            send_sem=y_send.at[u], recv_sem=y_recv.at[sem], device_id={"lower": who * 2 + core}, device_id_type=MESH,
        )

    units = [0, -1, 1, 2, -2, -3, 4, 3]
    wrote = {}
    fresh, running = [], []

    def root(u):
        return lax.rem(z + out * units[u] + 2 * N_Z, N_Y)

    def times(a, b):
        return lax.dot_general(a, b, (((0,), (0,)), ((), ())), preferred_element_type=F32)

    def m_product(u, d, p):
        value = times(m_piece(d, p)[...], upper[rows(m_row), :])
        if (u, p) in wrote:
            acc[u, p, :, pl.ds(0, n_u)] += value
        else:
            acc[u, p, :, pl.ds(0, n_u)] = value
        wrote[u, p] = True

    def e_full(u, d, p):
        value = times(e_piece(d, p)[...], upper_e[...])
        if (u, p) in wrote:
            acc[u, p, :, pl.ds(0, n_u)] += value[:, :n_u]
            acc[u, p, :, pl.ds(n_u, 2 * n_u)] = value[:, n_u:]
        else:
            acc[u, p] = value
        wrote[u, p] = True

    def stage(u, n):
        if n == 0:
            core_copy(u).start()
        elif n == 1:
            core_copy(u).wait_recv()
            half[u] = half[u] + acc[u, core]
            x1_copy(u, 0).start()
            x1_copy(u, 1).start()
        elif n == 2:
            x1_copy(u, 1).wait_recv()
            second_x[u] = half[u, block(x2)] + from_x1[u, 1]
            x2_copy(u).start()
            x1_copy(u, 0).wait_recv()
            quarter[u] = half[u, block(x)] + from_x1[u, 0]
        else:
            x2_copy(u).wait_recv()
            quarter[u] = quarter[u] + from_x2[u]
            who = root(u)

            @pl.when(who != y)
            def _():
                y_copy(u, y, y, who).start()

            @pl.when(who == y)
            def _():
                from_y[y] = quarter[u]

    def advance():
        for item in list(running):
            u, n = item
            stage(u, n)
            running.remove(item)
            if n < 3:
                fresh.append((u, n + 1))
        running.extend(fresh)
        fresh.clear()

    def begin(u):
        stage(u, 0)
        fresh.append((u, 1))

    def arrive(flow, onward=None):
        for p in (0, 1):
            ring(flow, p).wait_recv()
            if onward is not None:
                ring(onward, p).start()

    def e_arrive(d, onward=None, product=True):
        u = units.index(d + 8 if d < -3 else d)
        for p in (0, 1):
            ring(E_AT[d], p).wait_recv()
            if onward is not None:
                ring(onward, p).start()
            if product:
                e_full(u, d, p)

    def m_arrive(d, onward=None, onward2=None):
        u = units.index(d)
        for p in (0, 1):
            ring(M_AT[d], p).wait_recv()
            if onward is not None:
                ring(onward, p).start()
            m_product(u, d, p)

    arrive(PASS_U, FAR_U)
    send(E_AT[1])
    arrive(PASS_L, E_AT[2])
    send(M_AT[1])
    for p in (0, 1):
        m_product(0, 0, p)
    arrive(NEAR_U)
    arrive(FAR_U)
    for p in (0, 1):
        e_full(0, 0, p)
    begin(0)
    m_arrive(-1, M_AT[2])
    advance()
    e_arrive(1, M_AT[-2])
    advance()
    e_arrive(-1)
    begin(1)
    advance()
    e_arrive(2, M_AT[-3])
    advance()
    m_arrive(-2, M_AT[3])
    advance()
    m_arrive(1, E_AT[-2])
    begin(2)
    advance()
    m_arrive(-3, M_AT[4])
    advance()
    m_arrive(2, E_AT[-3])
    begin(3)
    advance()
    e_arrive(-2)
    begin(4)
    advance()
    m_arrive(3, E_AT[-4])
    advance()
    e_arrive(-3)
    begin(5)
    advance()
    m_arrive(4, E_AT[-5])
    advance()
    e_arrive(-4)
    begin(6)
    advance()
    e_arrive(-5)
    begin(7)
    advance()
    while running:
        advance()

    for k in range(1, N_Y):
        peer = lax.rem(y + k, N_Y)
        y_copy(0, peer, peer, peer).wait_recv()
    even = from_y[0] + from_y[2] + from_y[4] + from_y[6]
    odd = from_y[1] + from_y[3] + from_y[5] + from_y[7]
    sums[0] = even
    sums[1] = odd
    side = 2 * lax.rem(z, 2) - 1

    def z_copy(q, n):
        step = (side if q == 0 else -side) * n
        return pltpu.make_async_remote_copy(
            src_ref=sums.at[q, :, pl.ds(n * n_u, n_u)], dst_ref=from_z.at[q, n - 1],
            send_sem=z_send.at[q, n - 1], recv_sem=z_recv.at[q, n - 1], device_id=plane(step), device_id_type=MESH,
        )

    for n in (2, 1):
        for q in (0, 1):
            z_copy(q, n).start()
    total = even[:, :n_u] + odd[:, :n_u]
    for n in (1, 2):
        for q in (0, 1):
            z_copy(q, n).wait_recv()
            total = total + from_z[q, n - 1]
    out_ref[...] = total

    for flow in range(FLOWS):
        for p in (0, 1):
            ring(flow, p).wait_send()
    for u in range(len(units)):
        core_copy(u).wait_send()
        x1_copy(u, 0).wait_send()
        x1_copy(u, 1).wait_send()
        x2_copy(u).wait_send()
        who = root(u)

        @pl.when(who != y)
        def _():
            y_copy(u, y, y, who).wait_send()
    for n in (1, 2):
        for q in (0, 1):
            z_copy(q, n).wait_send()


def local(
    lower_vectors, upper_vectors, energy_lower, energy_upper, sym_lower, sym_upper, j_lower, j_upper
):
    rows, n_l = lower_vectors.shape[1:]
    n_u = upper_vectors.shape[2]
    n_out = n_l // (2 * N_X)
    depth = rows // SLICES
    vmem = pl.BlockSpec(memory_space=pltpu.VMEM)
    hbm = pl.BlockSpec(memory_space=pltpu.HBM)
    dma = pltpu.SemaphoreType.DMA
    kind = lower_vectors.dtype
    moments = pl.pallas_call(
        moments_kernel,
        out_shape=jax.ShapeDtypeStruct((n_out, n_u), F32),
        in_specs=[hbm, hbm],
        out_specs=vmem,
        scratch_shapes=[
            pltpu.VMEM((rows, n_l), kind),
            pltpu.VMEM((rows, n_u), kind),
            pltpu.VMEM((7, depth, n_l), kind),
            pltpu.VMEM((7, depth, n_l), kind),
            pltpu.VMEM((depth, n_l), kind),
            pltpu.VMEM((depth, n_u), kind),
            pltpu.VMEM((depth, 3 * n_u), kind),
            pltpu.VMEM((8, 2, n_l // 2, 3 * n_u), F32),
            pltpu.VMEM((8, n_l // 2, 3 * n_u), F32),
            pltpu.VMEM((8, 2, n_out, 3 * n_u), F32),
            pltpu.VMEM((8, n_out, 3 * n_u), F32),
            pltpu.VMEM((8, n_out, 3 * n_u), F32),
            pltpu.VMEM((8, n_out, 3 * n_u), F32),
            pltpu.VMEM((N_Y, n_out, 3 * n_u), F32),
            pltpu.VMEM((2, n_out, 3 * n_u), F32),
            pltpu.VMEM((2, 2, n_out, n_u), F32),
            dma((2,)),
            dma((FLOWS, 2)), dma((FLOWS, 2)),
            dma((8,)), dma((8,)),
            dma((8, 2)), dma((8, 2)),
            dma((8,)), dma((8,)),
            dma((8,)), dma((N_Y,)),
            dma((2, 2)), dma((2, 2)),
        ],
        compiler_params=pltpu.CompilerParams(
            collective_id=0, has_side_effects=True, vmem_limit_bytes=48 << 20
        ),
    )(lower_vectors[0], upper_vectors[0])
    parity = sym_lower % 2
    sym_rule = sym_upper[None, :] - sym_lower[:, None] == (1 - 2 * parity)[:, None]
    j_rule = jnp.abs(j_upper[None, :] - j_lower[:, None]) <= 1
    allowed = jnp.logical_and(sym_rule, j_rule)
    frequency = energy_upper[None, :] - energy_lower[:, None]
    weight_upper = (2 * j_upper + 1).astype(F32)
    value = frequency * frequency * frequency * (moments * moments) / weight_upper[None, :]
    return jnp.where(allowed, value, jnp.zeros_like(value))


def solution(mesh):
    return jax.shard_map(
        local,
        mesh=mesh,
        in_specs=(
            P("depth", "lower", "upper"),
            P("depth", "lower", "upper"),
            P(("lower", "depth")),
            P("upper"),
            P(("lower", "depth")),
            P("upper"),
            P(("lower", "depth")),
            P("upper"),
        ),
        out_specs=P(("lower", "depth"), "upper"),
        check_vma=False,
    )
```

time: 284 us -> 127 us (0.45)
  the two profiles are of different devices: /device:TPU:16 before, /device:TPU:8 now
where the time goes in v2:
time: 127 us
  Pallas kernels  122 us (96%)
  local copies, waits for them, and re-layouts  2.66 us (2%)
  other arithmetic  2.12 us (2%)
    pallas_call x1, Pallas kernels, local(): pl.pallas_call(moments_kernel, out_shape=jax.ShapeDtypeStruct((n_out, n_u...  122 us
    unnamed x16, local copies, waits for them, and re-layouts  2.66 us

profile of v2, /device:TPU:8, one launch (start us, length us, event | category | flops | bytes accessed | tf_op | source)
XLA Modules:
  0.0 127.2 jit_solution(2830164251145584966)
XLA Ops:
  0.0 0.0 copy-start.2
  0.0 0.0 copy-start.7
  0.0 0.0 copy-start.6
  0.0 0.0 copy-start.4
  0.0 0.0 copy-start.3
  0.0 0.0 copy-start.5
  0.0 0.7 fusion.5
  0.8 0.7 add_convert_fusion
  1.4 0.0 copy-start
  1.4 1.4 %copy-done = bf16[1,2048,384]{2,1,0:T(8,128)(2,1)S(1)} copy-done((bf16[1,2048,384]{2,1,0:T(8,128)(2,1)S(1)}, bf16[1,2048,384]{2,1,0:T(8,128)(2,1)}, u32[]{:S(2)}) %copy-start) | copy-done | bytes 1572888
  2.9 0.0 copy-start.1
  2.9 1.2 copy-done.1
  4.1 122.3 %shard_map.82 = f32[32,384]{1,0:T(8,128)S(1)} custom-call(bf16[2048,256]{1,0:T(8,128)(2,1)S(1)} %bitcast.3, bf16[2048,384]{1,0:T(8,128)(2,1)S(1)} %bitcast.2), custom_call_target="tpu_custom_call" | custom-call | tf_op jit(solution)/shard_map/pallas_call | solution.py:344
  126.4 0.0 copy-done.2
  126.4 0.0 copy-done.7
  126.4 0.0 copy-done.6
  126.4 0.0 copy-done.4
  126.4 0.0 copy-done.3
  126.5 0.0 copy-done.5
  126.5 0.7 fusion.2
Async XLA Ops:
  0.0 126.4 %copy-start.2 = (s32[384]{0:T(512)S(1)}, s32[384]{0:T(512)}, u32[]{:S(2)}) copy-start(s32[384]{0:T(512)} %param.15) | copy-start | bytes 4612
  0.0 126.4 %copy-start.7 = (s32[32]{0:T(128)S(1)}, s32[32]{0:T(128)}, u32[]{:S(2)}) copy-start(s32[32]{0:T(128)} %param.12) | copy-start | bytes 388
  0.0 126.4 %copy-start.6 = (s32[32]{0:T(128)S(1)}, s32[32]{0:T(128)}, u32[]{:S(2)}) copy-start(s32[32]{0:T(128)} %param.14) | copy-start | bytes 388
  0.0 126.4 %copy-start.4 = (s32[384]{0:T(512)S(1)}, s32[384]{0:T(512)}, u32[]{:S(2)}) copy-start(s32[384]{0:T(512)} %param.13) | copy-start | bytes 4612
  0.0 126.4 %copy-start.3 = (f32[384]{0:T(512)S(1)}, f32[384]{0:T(512)}, u32[]{:S(2)}) copy-start(f32[384]{0:T(512)} %param.11) | copy-start | bytes 4612
  0.0 126.4 %copy-start.5 = (f32[32]{0:T(128)S(1)}, f32[32]{0:T(128)}, u32[]{:S(2)}) copy-start(f32[32]{0:T(128)} %param.10) | copy-start | bytes 388
  1.4 1.4 %copy-start = (bf16[1,2048,384]{2,1,0:T(8,128)(2,1)S(1)}, bf16[1,2048,384]{2,1,0:T(8,128)(2,1)}, u32[]{:S(2)}) copy-start(bf16[1,2048,384]{2,1,0:T(8,128)(2,1)} %param.9) | copy-start | bytes 4718596
  2.9 1.2 copy-start.1

commit v3 on v1

--- a/solution.py
+++ b/solution.py
@@ -183,7 +183,7 @@
     n_u = upper_vectors.shape[2]
     n_out = n_l // (2 * n_x)
     vmem = pl.BlockSpec(memory_space=pltpu.VMEM)
-    hbm = pl.BlockSpec(memory_space=pl.ANY)
+    hbm = pl.BlockSpec(memory_space=pltpu.HBM)
     dma = pltpu.SemaphoreType.DMA
     moments = pl.pallas_call(
         functools.partial(moments_kernel, n_y=n_y, n_z=n_z, n_x=n_x),
@@ -206,7 +206,7 @@
             dma((n_z,)), dma((n_y,)),
         ],
         compiler_params=pltpu.CompilerParams(
-            collective_id=0, has_side_effects=True, vmem_limit_bytes=48 << 20
+            collective_id=0, has_side_effects=True, vmem_limit_bytes=60 << 20
         ),
     )(lower_vectors[0], upper_vectors[0])
     parity = sym_lower % 2

time: 115 us -> 114 us (level)
  local copies, waits for them, and re-layouts: 2.66 us -> 0.02 us
    unnamed x16 -> x12, local copies, waits for them, and re-layouts: 2.66 us -> 0.02 us
where the time goes in v3:
time: 114 us; the launch traced here: 113 us
  Pallas kernels  110 us (96%)
  other arithmetic  2.92 us (3%)
    pallas_call x1, Pallas kernels, local(): pl.pallas_call(functools.partial(moments_kernel, n_y=n_y, n_z=n_z, n_x=n_...  110 us

profile of v3, /device:TPU:24, one launch (start us, length us, event | category | flops | bytes accessed | tf_op | source)
XLA Modules:
  0.0 113.4 jit_solution(17308978370776128738)
XLA Ops:
  0.0 0.0 copy-start
  0.0 0.0 copy-start.5
  0.0 0.0 copy-start.4
  0.0 0.0 copy-start.2
  0.0 0.0 copy-start.1
  0.0 0.0 copy-start.3
  0.0 0.7 fusion.5
  0.8 0.7 add_convert_fusion
  1.4 110.4 %shard_map.82 = f32[32,384]{1,0:T(8,128)} custom-call(bf16[2048,256]{1,0:T(8,128)(2,1)} %bitcast.3, bf16[2048,384]{1,0:T(8,128)(2,1)} %bitcast.2), custom_call_target="tpu_custom_call" | custom-call | tf_op jit(solution)/shard_map/pallas_call | solution.py:188
  111.8 0.0 copy-done
  111.8 0.0 copy-done.5
  111.8 0.0 copy-done.4
  111.8 0.0 copy-done.2
  111.9 0.0 copy-done.1
  111.9 0.0 copy-done.3
  111.9 1.5 %fusion.2 = f32[32,384]{1,0:T(8,128)} fusion(f32[32,384]{1,0:T(8,128)} %shard_map.82, f32[384]{0:T(512)S(1)} %add_convert_fusion, f32[32]{0:T(128)S(1)} %copy-done.3, f32[384]{0:T(512)S(1)} %copy-done.1, s32[32]{0:T(128)S(1)} %copy-done.4, s32[384]{0:T(512)S(1)} %copy-done, s32[32]{0:T(128)S(1)} %fusion.5, s32[32]{0:T(128)S(1)} %copy-done.5, s32[384]{0:T(512)S(1)} %copy-done.2), kind=kLoop, calls=%fused_computation.3 | loop fusion | flops 159744 | bytes 104960 | tf_op jit(solution)/shard_map/jit(_where)/select_n | solution.py:219
Async XLA Ops:
  0.0 111.8 %copy-start = (s32[384]{0:T(512)S(1)}, s32[384]{0:T(512)}, u32[]{:S(2)}) copy-start(s32[384]{0:T(512)} %param.15) | copy-start | bytes 4612
  0.0 111.8 %copy-start.5 = (s32[32]{0:T(128)S(1)}, s32[32]{0:T(128)}, u32[]{:S(2)}) copy-start(s32[32]{0:T(128)} %param.12) | copy-start | bytes 388
  0.0 111.8 %copy-start.4 = (s32[32]{0:T(128)S(1)}, s32[32]{0:T(128)}, u32[]{:S(2)}) copy-start(s32[32]{0:T(128)} %param.14) | copy-start | bytes 388
  0.0 111.8 %copy-start.2 = (s32[384]{0:T(512)S(1)}, s32[384]{0:T(512)}, u32[]{:S(2)}) copy-start(s32[384]{0:T(512)} %param.13) | copy-start | bytes 4612
  0.0 111.8 %copy-start.1 = (f32[384]{0:T(512)S(1)}, f32[384]{0:T(512)}, u32[]{:S(2)}) copy-start(f32[384]{0:T(512)} %param.11) | copy-start | bytes 4612
  0.0 111.8 %copy-start.3 = (f32[32]{0:T(128)S(1)}, f32[32]{0:T(128)}, u32[]{:S(2)}) copy-start(f32[32]{0:T(128)} %param.10) | copy-start | bytes 388

commit v4 on v2

--- a/solution.py
+++ b/solution.py
@@ -18,14 +18,52 @@
 M_AT = {1: 7, 2: 8, 3: 9, 4: 10, -1: 11, -2: 12, -3: 13}
 PASS_L, NEAR_U, FAR_U, PASS_U = 14, 15, 16, 17
 FLOWS = 18
+HOPS = (
+    (M_AT, -1, M_AT[2]), (E_AT, 1, M_AT[-2]), (E_AT, -1, None), (E_AT, 2, M_AT[-3]), (M_AT, -2, M_AT[3]),
+    (M_AT, 1, E_AT[-2]), (M_AT, -3, M_AT[4]), (M_AT, 2, E_AT[-3]), (E_AT, -2, None), (M_AT, 3, E_AT[-4]),
+    (E_AT, -3, None), (M_AT, 4, E_AT[-5]), (E_AT, -4, None), (E_AT, -5, None),
+)
+LAST = 7
+PLAN = (
+    (),
+    ((0, 1),),
+    (),
+    (),
+    (),
+    (),
+    (),
+    ((0, 2), (1, 1)),
+    (),
+    ((0, 3),),
+    (),
+    (),
+    (),
+    ((1, 2), (2, 1)),
+    (),
+    ((0, 4), (1, 3)),
+    (),
+    ((3, 1), (2, 2)),
+    (),
+    ((1, 4),),
+    (),
+    ((4, 1), (3, 2)),
+    (),
+    ((2, 3), (5, 1)),
+    (),
+    ((4, 2),),
+    ((3, 3), (2, 4), (6, 1)),
+    ((5, 2), (4, 3)),
+    (),
+    ((3, 4), (6, 2), (5, 3), (4, 4), (7, 3), (5, 4), (6, 3), (7, 4), (6, 4)),
+)
 
 
 def moments_kernel(
     lower_hbm, upper_hbm, out_ref,
     lower, upper, e_block, m_block, pass_l, pass_u, upper_e,
-    acc, half, from_x1, second_x, from_x2, quarter, from_y, sums, from_z,
+    acc, half, from_x1, second_x, from_x2, quarter, from_xd, from_y, part, finals,
     load_sem, ring_send, ring_recv, core_send, core_recv, x1_send, x1_recv, x2_send, x2_recv, y_send, y_recv,
-    z_send, z_recv,
+    xd_send, xd_recv, final_send, final_recv,
 ):
     li, z, x = lax.axis_index("lower"), lax.axis_index("upper"), lax.axis_index("depth")
     y, core = li // 2, lax.rem(li, 2)
@@ -33,6 +71,7 @@
     n_l, n_u = lower.shape[1], upper.shape[1]
     wide = n_l // 2
     n_out = wide // N_X
+    n_group = n_out // 4
 
     place = lax.rem(z + lax.rem(y, 2), N_Z)
     out = 2 * lax.rem(place, 2) - 1
@@ -60,8 +99,13 @@
     load_lower.start()
 
     barrier = pltpu.get_barrier_semaphore()
-    partners = [plane(s) for s in (1, -1, 2, -2)] + [sibling, {"depth": flip}, {"depth": mirror}]
-    partners += [{"lower": lax.rem(y + k, N_Y) * 2 + core} for k in range(1, N_Y)]
+    side = 2 * lax.rem(z, 2) - 1
+    partners = [inner, sibling] + [{"depth": lax.rem(x + k, N_X)} for k in range(1, N_X)]
+    for k in range(N_Y):
+        peer = lax.rem(y + k, N_Y)
+        at = side * (1 - 2 * lax.rem(peer, 2))
+        for step in (0, at, -2 * at) if k else (at, -2 * at):
+            partners.append({"lower": peer * 2 + core, "upper": lax.rem(z + step + 2 * N_Z, N_Z)})
     for who in partners:
         pl.semaphore_signal(barrier, inc=1, device_id=who, device_id_type=MESH)
     pl.semaphore_wait(barrier, len(partners))
@@ -125,6 +169,9 @@
             send_sem=core_send.at[u], recv_sem=core_recv.at[u], device_id=sibling, device_id_type=MESH,
         )
 
+    def group(k):
+        return pl.ds(pl.multiple_of(k * n_group, n_group), n_group)
+
     def block(k):
         return pl.ds(pl.multiple_of(k * n_out, n_out), n_out)
 
@@ -140,15 +187,31 @@
             send_sem=x2_send.at[u], recv_sem=x2_recv.at[u], device_id={"depth": x2}, device_id_type=MESH,
         )
 
-    def y_copy(u, sem, slot, who):
-        return pltpu.make_async_remote_copy(
-            src_ref=quarter.at[u], dst_ref=from_y.at[slot],
-            send_sem=y_send.at[u], recv_sem=y_recv.at[sem], device_id={"lower": who * 2 + core}, device_id_type=MESH,
+    def y_copy(u, k):
+        to = lax.rem(y + 2 * k, N_Y)
+        return pltpu.make_async_remote_copy(
+            src_ref=quarter.at[u, group(to // 2)], dst_ref=from_y.at[u, k - 1],
+            send_sem=y_send.at[u, k - 1], recv_sem=y_recv.at[u, k - 1], device_id={"lower": to * 2 + core},
+            device_id_type=MESH,
+        )
+
+    def xd_copy(k):
+        to = lax.rem(x + k, N_X)
+        return pltpu.make_async_remote_copy(
+            src_ref=half.at[LAST, block(to)], dst_ref=from_xd.at[k - 1],
+            send_sem=xd_send.at[k - 1], recv_sem=xd_recv.at[k - 1], device_id={"depth": to}, device_id_type=MESH,
+        )
+
+    def final_copy(u, j, who, of):
+        step = j * out
+        return pltpu.make_async_remote_copy(
+            src_ref=part.at[u, j], dst_ref=finals.at[j, lax.rem(of, 2), group(of // 2)],
+            send_sem=final_send.at[u, j], recv_sem=final_recv.at[j, of],
+            device_id={"lower": who * 2 + core, "upper": lax.rem(z + step + 2 * N_Z, N_Z)}, device_id_type=MESH,
         )
 
     units = [0, -1, 1, 2, -2, -3, 4, 3]
     wrote = {}
-    fresh, running = [], []
 
     def root(u):
         return lax.rem(z + out * units[u] + 2 * N_Z, N_Y)
@@ -179,63 +242,58 @@
         elif n == 1:
             core_copy(u).wait_recv()
             half[u] = half[u] + acc[u, core]
-            x1_copy(u, 0).start()
-            x1_copy(u, 1).start()
+            if u == LAST:
+                for k in (1, 3, 2):
+                    xd_copy(k).start()
+            else:
+                x1_copy(u, 1).start()
+                x1_copy(u, 0).start()
         elif n == 2:
             x1_copy(u, 1).wait_recv()
             second_x[u] = half[u, block(x2)] + from_x1[u, 1]
             x2_copy(u).start()
             x1_copy(u, 0).wait_recv()
             quarter[u] = half[u, block(x)] + from_x1[u, 0]
+        elif n == 3:
+            if u == LAST:
+                value = half[u, block(x)]
+                for k in (1, 3, 2):
+                    xd_copy(k).wait_recv()
+                    value = value + from_xd[k - 1]
+                quarter[u] = value
+            else:
+                x2_copy(u).wait_recv()
+                quarter[u] = quarter[u] + from_x2[u]
+            for k in (2, 1, 3):
+                y_copy(u, k).start()
         else:
-            x2_copy(u).wait_recv()
-            quarter[u] = quarter[u] + from_x2[u]
+            value = quarter[u, group(y // 2)]
+            for k in (1, 3, 2):
+                y_copy(u, k).wait_recv()
+                value = value + from_y[u, k - 1]
+            for j in range(3):
+                part[u, j] = value[:, j * n_u : (j + 1) * n_u]
             who = root(u)
+            final_copy(u, 2, who, y).start()
+            final_copy(u, 1, who, y).start()
 
             @pl.when(who != y)
             def _():
-                y_copy(u, y, y, who).start()
+                final_copy(u, 0, who, y).start()
 
             @pl.when(who == y)
             def _():
-                from_y[y] = quarter[u]
-
-    def advance():
-        for item in list(running):
-            u, n = item
-            stage(u, n)
-            running.remove(item)
-            if n < 3:
-                fresh.append((u, n + 1))
-        running.extend(fresh)
-        fresh.clear()
-
-    def begin(u):
-        stage(u, 0)
-        fresh.append((u, 1))
+                finals[0, lax.rem(y, 2), group(y // 2)] = part[u, 0]
+
+    def due(n):
+        for u, k in PLAN[n]:
+            stage(u, k)
 
     def arrive(flow, onward=None):
         for p in (0, 1):
             ring(flow, p).wait_recv()
             if onward is not None:
                 ring(onward, p).start()
-
-    def e_arrive(d, onward=None, product=True):
-        u = units.index(d + 8 if d < -3 else d)
-        for p in (0, 1):
-            ring(E_AT[d], p).wait_recv()
-            if onward is not None:
-                ring(onward, p).start()
-            if product:
-                e_full(u, d, p)
-
-    def m_arrive(d, onward=None, onward2=None):
-        u = units.index(d)
-        for p in (0, 1):
-            ring(M_AT[d], p).wait_recv()
-            if onward is not None:
-                ring(onward, p).start()
-            m_product(u, d, p)
 
     arrive(PASS_U, FAR_U)
     send(E_AT[1])
@@ -247,69 +305,35 @@
     arrive(FAR_U)
     for p in (0, 1):
         e_full(0, 0, p)
-    begin(0)
-    m_arrive(-1, M_AT[2])
-    advance()
-    e_arrive(1, M_AT[-2])
-    advance()
-    e_arrive(-1)
-    begin(1)
-    advance()
-    e_arrive(2, M_AT[-3])
-    advance()
-    m_arrive(-2, M_AT[3])
-    advance()
-    m_arrive(1, E_AT[-2])
-    begin(2)
-    advance()
-    m_arrive(-3, M_AT[4])
-    advance()
-    m_arrive(2, E_AT[-3])
-    begin(3)
-    advance()
-    e_arrive(-2)
-    begin(4)
-    advance()
-    m_arrive(3, E_AT[-4])
-    advance()
-    e_arrive(-3)
-    begin(5)
-    advance()
-    m_arrive(4, E_AT[-5])
-    advance()
-    e_arrive(-4)
-    begin(6)
-    advance()
-    e_arrive(-5)
-    begin(7)
-    advance()
-    while running:
-        advance()
-
-    for k in range(1, N_Y):
-        peer = lax.rem(y + k, N_Y)
-        y_copy(0, peer, peer, peer).wait_recv()
-    even = from_y[0] + from_y[2] + from_y[4] + from_y[6]
-    odd = from_y[1] + from_y[3] + from_y[5] + from_y[7]
-    sums[0] = even
-    sums[1] = odd
-    side = 2 * lax.rem(z, 2) - 1
-
-    def z_copy(q, n):
-        step = (side if q == 0 else -side) * n
-        return pltpu.make_async_remote_copy(
-            src_ref=sums.at[q, :, pl.ds(n * n_u, n_u)], dst_ref=from_z.at[q, n - 1],
-            send_sem=z_send.at[q, n - 1], recv_sem=z_recv.at[q, n - 1], device_id=plane(step), device_id_type=MESH,
-        )
-
-    for n in (2, 1):
-        for q in (0, 1):
-            z_copy(q, n).start()
-    total = even[:, :n_u] + odd[:, :n_u]
-    for n in (1, 2):
-        for q in (0, 1):
-            z_copy(q, n).wait_recv()
-            total = total + from_z[q, n - 1]
+    stage(0, 0)
+    due(0)
+    for n, (kind, d, onward) in enumerate(HOPS):
+        u = units.index(d + 8 if d < -3 else d)
+        for p in (0, 1):
+            ring(kind[d], p).wait_recv()
+            if onward is not None:
+                ring(onward, p).start()
+            done = (u, p) in wrote
+            if kind is E_AT:
+                e_full(u, d, p)
+            else:
+                m_product(u, d, p)
+            if u == LAST and done:
+                pl.when(core == 1 - p)(functools.partial(stage, u, 0))
+            elif done and p == 1:
+                stage(u, 0)
+            due(2 * n + p + 1)
+            if u == LAST and done:
+                pl.when(core == p)(functools.partial(stage, u, 1))
+    due(2 * len(HOPS) + 1)
+
+    for j in range(3):
+        for k in range(1 if j == 0 else 0, N_Y):
+            peer = lax.rem(y + k, N_Y)
+            final_copy(0, j, peer, peer).wait_recv()
+    total = finals[0, 0] + finals[0, 1]
+    for j in (1, 2):
+        total = total + (finals[j, 0] + finals[j, 1])
     out_ref[...] = total
 
     for flow in range(FLOWS):
@@ -317,17 +341,22 @@
             ring(flow, p).wait_send()
     for u in range(len(units)):
         core_copy(u).wait_send()
-        x1_copy(u, 0).wait_send()
-        x1_copy(u, 1).wait_send()
-        x2_copy(u).wait_send()
+        if u == LAST:
+            for k in (1, 2, 3):
+                xd_copy(k).wait_send()
+        else:
+            x1_copy(u, 0).wait_send()
+            x1_copy(u, 1).wait_send()
+            x2_copy(u).wait_send()
+        for k in (1, 2, 3):
+            y_copy(u, k).wait_send()
         who = root(u)
+        final_copy(u, 1, who, y).wait_send()
+        final_copy(u, 2, who, y).wait_send()
 
         @pl.when(who != y)
         def _():
-            y_copy(u, y, y, who).wait_send()
-    for n in (1, 2):
-        for q in (0, 1):
-            z_copy(q, n).wait_send()
+            final_copy(u, 0, who, y).wait_send()
 
 
 def local(
@@ -360,19 +389,21 @@
             pltpu.VMEM((8, n_out, 3 * n_u), F32),
             pltpu.VMEM((8, n_out, 3 * n_u), F32),
             pltpu.VMEM((8, n_out, 3 * n_u), F32),
-            pltpu.VMEM((N_Y, n_out, 3 * n_u), F32),
-            pltpu.VMEM((2, n_out, 3 * n_u), F32),
-            pltpu.VMEM((2, 2, n_out, n_u), F32),
+            pltpu.VMEM((3, n_out, 3 * n_u), F32),
+            pltpu.VMEM((8, 3, n_out // 4, 3 * n_u), F32),
+            pltpu.VMEM((8, 3, n_out // 4, n_u), F32),
+            pltpu.VMEM((3, 2, n_out, n_u), F32),
             dma((2,)),
             dma((FLOWS, 2)), dma((FLOWS, 2)),
             dma((8,)), dma((8,)),
             dma((8, 2)), dma((8, 2)),
             dma((8,)), dma((8,)),
-            dma((8,)), dma((N_Y,)),
-            dma((2, 2)), dma((2, 2)),
+            dma((8, 3)), dma((8, 3)),
+            dma((3,)), dma((3,)),
+            dma((8, 3)), dma((3, N_Y)),
         ],
         compiler_params=pltpu.CompilerParams(
-            collective_id=0, has_side_effects=True, vmem_limit_bytes=48 << 20
+            collective_id=0, has_side_effects=True, vmem_limit_bytes=60 << 20
         ),
     )(lower_vectors[0], upper_vectors[0])
     parity = sym_lower % 2

time: 127 us -> 110 us (0.87)
  the two profiles are of different devices: /device:TPU:8 before, /device:TPU:40 now
where the time goes in v4:
time: 110 us
  Pallas kernels  107 us (97%)
  other arithmetic  2.92 us (3%)
    pallas_call x1, Pallas kernels, local(): pl.pallas_call(moments_kernel, out_shape=jax.ShapeDtypeStruct((n_out, n_u...  107 us

profile of v4, /device:TPU:40, one launch (start us, length us, event | category | flops | bytes accessed | tf_op | source)
XLA Modules:
  0.0 109.7 jit_solution(13814414325626459754)
XLA Ops:
  0.0 0.0 copy-start
  0.0 0.0 copy-start.5
  0.0 0.0 copy-start.4
  0.0 0.0 copy-start.2
  0.0 0.0 copy-start.1
  0.0 0.0 copy-start.3
  0.0 0.7 fusion.5
  0.8 0.7 add_convert_fusion
  1.4 106.6 %shard_map.82 = f32[32,384]{1,0:T(8,128)} custom-call(bf16[2048,256]{1,0:T(8,128)(2,1)} %bitcast.3, bf16[2048,384]{1,0:T(8,128)(2,1)} %bitcast.2), custom_call_target="tpu_custom_call" | custom-call | tf_op jit(solution)/shard_map/pallas_call | solution.py:373
  108.1 0.0 copy-done
  108.1 0.0 copy-done.5
  108.1 0.0 copy-done.4
  108.1 0.0 copy-done.2
  108.1 0.0 copy-done.1
  108.1 0.0 copy-done.3
  108.2 1.5 %fusion.2 = f32[32,384]{1,0:T(8,128)} fusion(f32[32,384]{1,0:T(8,128)} %shard_map.82, f32[384]{0:T(512)S(1)} %add_convert_fusion, f32[32]{0:T(128)S(1)} %copy-done.3, f32[384]{0:T(512)S(1)} %copy-done.1, s32[32]{0:T(128)S(1)} %copy-done.4, s32[384]{0:T(512)S(1)} %copy-done, s32[32]{0:T(128)S(1)} %fusion.5, s32[32]{0:T(128)S(1)} %copy-done.5, s32[384]{0:T(512)S(1)} %copy-done.2), kind=kLoop, calls=%fused_computation.3 | loop fusion | flops 159744 | bytes 104960 | tf_op jit(solution)/shard_map/jit(_where)/select_n | solution.py:416
Async XLA Ops:
  0.0 108.1 %copy-start = (s32[384]{0:T(512)S(1)}, s32[384]{0:T(512)}, u32[]{:S(2)}) copy-start(s32[384]{0:T(512)} %param.15) | copy-start | bytes 4612
  0.0 108.1 %copy-start.5 = (s32[32]{0:T(128)S(1)}, s32[32]{0:T(128)}, u32[]{:S(2)}) copy-start(s32[32]{0:T(128)} %param.12) | copy-start | bytes 388
  0.0 108.1 %copy-start.4 = (s32[32]{0:T(128)S(1)}, s32[32]{0:T(128)}, u32[]{:S(2)}) copy-start(s32[32]{0:T(128)} %param.14) | copy-start | bytes 388
  0.0 108.1 %copy-start.2 = (s32[384]{0:T(512)S(1)}, s32[384]{0:T(512)}, u32[]{:S(2)}) copy-start(s32[384]{0:T(512)} %param.13) | copy-start | bytes 4612
  0.0 108.1 %copy-start.1 = (f32[384]{0:T(512)S(1)}, f32[384]{0:T(512)}, u32[]{:S(2)}) copy-start(f32[384]{0:T(512)} %param.11) | copy-start | bytes 4612
  0.0 108.1 %copy-start.3 = (f32[32]{0:T(128)S(1)}, f32[32]{0:T(128)}, u32[]{:S(2)}) copy-start(f32[32]{0:T(128)} %param.10) | copy-start | bytes 388

commit v5 on v4

--- a/solution.py
+++ b/solution.py
@@ -19,11 +19,12 @@
 PASS_L, NEAR_U, FAR_U, PASS_U = 14, 15, 16, 17
 FLOWS = 18
 HOPS = (
-    (M_AT, -1, M_AT[2]), (E_AT, 1, M_AT[-2]), (E_AT, -1, None), (E_AT, 2, M_AT[-3]), (M_AT, -2, M_AT[3]),
-    (M_AT, 1, E_AT[-2]), (M_AT, -3, M_AT[4]), (M_AT, 2, E_AT[-3]), (E_AT, -2, None), (M_AT, 3, E_AT[-4]),
+    (M_AT, -1, M_AT[2]), (E_AT, 1, M_AT[-2]), (E_AT, -1, None), (M_AT, 1, E_AT[-2]), (M_AT, -2, M_AT[3]),
+    (E_AT, 2, M_AT[-3]), (E_AT, -2, None), (M_AT, 2, E_AT[-3]), (M_AT, -3, M_AT[4]), (M_AT, 3, E_AT[-4]),
     (E_AT, -3, None), (M_AT, 4, E_AT[-5]), (E_AT, -4, None), (E_AT, -5, None),
 )
-LAST = 7
+DIRECT = (6, 7)
+SPLIT = (1, 2, 3, 4, 5, 6, 7)
 PLAN = (
     (),
     ((0, 1),),
@@ -32,29 +33,29 @@
     (),
     (),
     (),
-    ((0, 2), (1, 1)),
+    ((0, 2),),
+    (),
+    (),
     (),
     ((0, 3),),
     (),
-    (),
-    (),
-    ((1, 2), (2, 1)),
-    (),
-    ((0, 4), (1, 3)),
-    (),
-    ((3, 1), (2, 2)),
-    (),
-    ((1, 4),),
-    (),
-    ((4, 1), (3, 2)),
-    (),
-    ((2, 3), (5, 1)),
-    (),
-    ((4, 2),),
-    ((3, 3), (2, 4), (6, 1)),
-    ((5, 2), (4, 3)),
-    (),
-    ((3, 4), (6, 2), (5, 3), (4, 4), (7, 3), (5, 4), (6, 3), (7, 4), (6, 4)),
+    ((1, 2),),
+    (),
+    ((0, 4), (2, 2)),
+    (),
+    ((1, 3),),
+    (),
+    ((2, 3),),
+    (),
+    ((1, 4), (3, 2)),
+    (),
+    ((2, 4), (4, 2)),
+    (),
+    ((3, 3),),
+    ((4, 3),),
+    ((3, 4), (5, 2)),
+    (),
+    ((4, 4), (6, 3), (5, 3), (6, 4), (7, 3), (5, 4), (7, 4)),
 )
 
 
@@ -195,11 +196,11 @@
             device_id_type=MESH,
         )
 
-    def xd_copy(k):
+    def xd_copy(u, k):
         to = lax.rem(x + k, N_X)
         return pltpu.make_async_remote_copy(
-            src_ref=half.at[LAST, block(to)], dst_ref=from_xd.at[k - 1],
-            send_sem=xd_send.at[k - 1], recv_sem=xd_recv.at[k - 1], device_id={"depth": to}, device_id_type=MESH,
+            src_ref=half.at[u, block(to)], dst_ref=from_xd.at[u, k - 1],
+            send_sem=xd_send.at[u, k - 1], recv_sem=xd_recv.at[u, k - 1], device_id={"depth": to}, device_id_type=MESH,
         )
 
     def final_copy(u, j, who, of):
@@ -210,7 +211,7 @@
             device_id={"lower": who * 2 + core, "upper": lax.rem(z + step + 2 * N_Z, N_Z)}, device_id_type=MESH,
         )
 
-    units = [0, -1, 1, 2, -2, -3, 4, 3]
+    units = [0, -1, 1, -2, 2, -3, 4, 3]
     wrote = {}
 
     def root(u):
@@ -242,9 +243,9 @@
         elif n == 1:
             core_copy(u).wait_recv()
             half[u] = half[u] + acc[u, core]
-            if u == LAST:
+            if u in DIRECT:
                 for k in (1, 3, 2):
-                    xd_copy(k).start()
+                    xd_copy(u, k).start()
             else:
                 x1_copy(u, 1).start()
                 x1_copy(u, 0).start()
@@ -255,11 +256,11 @@
             x1_copy(u, 0).wait_recv()
             quarter[u] = half[u, block(x)] + from_x1[u, 0]
         elif n == 3:
-            if u == LAST:
+            if u in DIRECT:
                 value = half[u, block(x)]
                 for k in (1, 3, 2):
-                    xd_copy(k).wait_recv()
-                    value = value + from_xd[k - 1]
+                    xd_copy(u, k).wait_recv()
+                    value = value + from_xd[u, k - 1]
                 quarter[u] = value
             else:
                 x2_copy(u).wait_recv()
@@ -297,8 +298,8 @@
 
     arrive(PASS_U, FAR_U)
     send(E_AT[1])
+    send(M_AT[1])
     arrive(PASS_L, E_AT[2])
-    send(M_AT[1])
     for p in (0, 1):
         m_product(0, 0, p)
     arrive(NEAR_U)
@@ -318,12 +319,12 @@
                 e_full(u, d, p)
             else:
                 m_product(u, d, p)
-            if u == LAST and done:
+            if u in SPLIT and done:
                 pl.when(core == 1 - p)(functools.partial(stage, u, 0))
             elif done and p == 1:
                 stage(u, 0)
             due(2 * n + p + 1)
-            if u == LAST and done:
+            if u in SPLIT and done:
                 pl.when(core == p)(functools.partial(stage, u, 1))
     due(2 * len(HOPS) + 1)
 
@@ -341,9 +342,9 @@
             ring(flow, p).wait_send()
     for u in range(len(units)):
         core_copy(u).wait_send()
-        if u == LAST:
+        if u in DIRECT:
             for k in (1, 2, 3):
-                xd_copy(k).wait_send()
+                xd_copy(u, k).wait_send()
         else:
             x1_copy(u, 0).wait_send()
             x1_copy(u, 1).wait_send()
@@ -389,7 +390,7 @@
             pltpu.VMEM((8, n_out, 3 * n_u), F32),
             pltpu.VMEM((8, n_out, 3 * n_u), F32),
             pltpu.VMEM((8, n_out, 3 * n_u), F32),
-            pltpu.VMEM((3, n_out, 3 * n_u), F32),
+            pltpu.VMEM((8, 3, n_out, 3 * n_u), F32),
             pltpu.VMEM((8, 3, n_out // 4, 3 * n_u), F32),
             pltpu.VMEM((8, 3, n_out // 4, n_u), F32),
             pltpu.VMEM((3, 2, n_out, n_u), F32),
@@ -399,7 +400,7 @@
             dma((8, 2)), dma((8, 2)),
             dma((8,)), dma((8,)),
             dma((8, 3)), dma((8, 3)),
-            dma((3,)), dma((3,)),
+            dma((8, 3)), dma((8, 3)),
             dma((8, 3)), dma((3, N_Y)),
         ],
         compiler_params=pltpu.CompilerParams(

time: 110 us -> 109 us (level)
  the two profiles are of different devices: /device:TPU:40 before, /device:TPU:16 now
where the time goes in v5:
time: 109 us; the launch traced here: 108 us
  Pallas kernels  105 us (96%)
  other arithmetic  2.92 us (3%)
    pallas_call x1, Pallas kernels, local(): pl.pallas_call(moments_kernel, out_shape=jax.ShapeDtypeStruct((n_out, n_u...  105 us

profile of v5, /device:TPU:16, one launch (start us, length us, event | category | flops | bytes accessed | tf_op | source)
XLA Modules:
  0.0 108.4 jit_solution(13027897236719796555)
XLA Ops:
  0.0 0.0 copy-start
  0.0 0.0 copy-start.5
  0.0 0.0 copy-start.4
  0.0 0.0 copy-start.2
  0.0 0.0 copy-start.1
  0.0 0.0 copy-start.3
  0.0 0.7 fusion.5
  0.8 0.7 add_convert_fusion
  1.4 105.4 %shard_map.82 = f32[32,384]{1,0:T(8,128)} custom-call(bf16[2048,256]{1,0:T(8,128)(2,1)} %bitcast.3, bf16[2048,384]{1,0:T(8,128)(2,1)} %bitcast.2), custom_call_target="tpu_custom_call" | custom-call | tf_op jit(solution)/shard_map/pallas_call | solution.py:374
  106.8 0.0 copy-done
  106.8 0.0 copy-done.5
  106.8 0.0 copy-done.4
  106.9 0.0 copy-done.2
  106.9 0.0 copy-done.1
  106.9 0.0 copy-done.3
  106.9 1.5 %fusion.2 = f32[32,384]{1,0:T(8,128)} fusion(f32[32,384]{1,0:T(8,128)} %shard_map.82, f32[384]{0:T(512)S(1)} %add_convert_fusion, f32[32]{0:T(128)S(1)} %copy-done.3, f32[384]{0:T(512)S(1)} %copy-done.1, s32[32]{0:T(128)S(1)} %copy-done.4, s32[384]{0:T(512)S(1)} %copy-done, s32[32]{0:T(128)S(1)} %fusion.5, s32[32]{0:T(128)S(1)} %copy-done.5, s32[384]{0:T(512)S(1)} %copy-done.2), kind=kLoop, calls=%fused_computation.3 | loop fusion | flops 159744 | bytes 104960 | tf_op jit(solution)/shard_map/jit(_where)/select_n | solution.py:417
Async XLA Ops:
  0.0 106.8 %copy-start = (s32[384]{0:T(512)S(1)}, s32[384]{0:T(512)}, u32[]{:S(2)}) copy-start(s32[384]{0:T(512)} %param.15) | copy-start | bytes 4612
  0.0 106.8 %copy-start.5 = (s32[32]{0:T(128)S(1)}, s32[32]{0:T(128)}, u32[]{:S(2)}) copy-start(s32[32]{0:T(128)} %param.12) | copy-start | bytes 388
  0.0 106.8 %copy-start.4 = (s32[32]{0:T(128)S(1)}, s32[32]{0:T(128)}, u32[]{:S(2)}) copy-start(s32[32]{0:T(128)} %param.14) | copy-start | bytes 388
  0.0 106.9 %copy-start.2 = (s32[384]{0:T(512)S(1)}, s32[384]{0:T(512)}, u32[]{:S(2)}) copy-start(s32[384]{0:T(512)} %param.13) | copy-start | bytes 4612
  0.0 106.9 %copy-start.1 = (f32[384]{0:T(512)S(1)}, f32[384]{0:T(512)}, u32[]{:S(2)}) copy-start(f32[384]{0:T(512)} %param.11) | copy-start | bytes 4612
  0.0 106.9 %copy-start.3 = (f32[32]{0:T(128)S(1)}, f32[32]{0:T(128)}, u32[]{:S(2)}) copy-start(f32[32]{0:T(128)} %param.10) | copy-start | bytes 388

commit v6 on v5

--- a/solution.py
+++ b/solution.py
@@ -55,7 +55,7 @@
     ((4, 3),),
     ((3, 4), (5, 2)),
     (),
-    ((4, 4), (6, 3), (5, 3), (6, 4), (7, 3), (5, 4), (7, 4)),
+    ((6, 3), (5, 3), (4, 4), (7, 3), (6, 4), (5, 4), (7, 4)),
 )
 
 

time: 109 us -> 108 us (level)
  no operation moved by 1% of the time
where the time goes in v6:
time: 108 us
  Pallas kernels  105 us (97%)
  other arithmetic  2.92 us (3%)
    pallas_call x1, Pallas kernels, local(): pl.pallas_call(moments_kernel, out_shape=jax.ShapeDtypeStruct((n_out, n_u...  105 us

profile of v6, /device:TPU:16, one launch (start us, length us, event | category | flops | bytes accessed | tf_op | source)
XLA Modules:
  0.0 107.6 jit_solution(12581901830505257063)
XLA Ops:
  0.0 0.0 copy-start
  0.0 0.0 copy-start.5
  0.0 0.0 copy-start.4
  0.0 0.0 copy-start.2
  0.0 0.0 copy-start.1
  0.0 0.0 copy-start.3
  0.0 0.7 fusion.5
  0.8 0.7 add_convert_fusion
  1.4 104.5 %shard_map.82 = f32[32,384]{1,0:T(8,128)} custom-call(bf16[2048,256]{1,0:T(8,128)(2,1)} %bitcast.3, bf16[2048,384]{1,0:T(8,128)(2,1)} %bitcast.2), custom_call_target="tpu_custom_call" | custom-call | tf_op jit(solution)/shard_map/pallas_call | solution.py:374
  106.0 0.0 copy-done
  106.0 0.0 copy-done.5
  106.0 0.0 copy-done.4
  106.0 0.0 copy-done.2
  106.0 0.0 copy-done.1
  106.0 0.0 copy-done.3
  106.0 1.5 %fusion.2 = f32[32,384]{1,0:T(8,128)} fusion(f32[32,384]{1,0:T(8,128)} %shard_map.82, f32[384]{0:T(512)S(1)} %add_convert_fusion, f32[32]{0:T(128)S(1)} %copy-done.3, f32[384]{0:T(512)S(1)} %copy-done.1, s32[32]{0:T(128)S(1)} %copy-done.4, s32[384]{0:T(512)S(1)} %copy-done, s32[32]{0:T(128)S(1)} %fusion.5, s32[32]{0:T(128)S(1)} %copy-done.5, s32[384]{0:T(512)S(1)} %copy-done.2), kind=kLoop, calls=%fused_computation.3 | loop fusion | flops 159744 | bytes 104960 | tf_op jit(solution)/shard_map/jit(_where)/select_n | solution.py:417
Async XLA Ops:
  0.0 106.0 %copy-start = (s32[384]{0:T(512)S(1)}, s32[384]{0:T(512)}, u32[]{:S(2)}) copy-start(s32[384]{0:T(512)} %param.15) | copy-start | bytes 4612
  0.0 106.0 %copy-start.5 = (s32[32]{0:T(128)S(1)}, s32[32]{0:T(128)}, u32[]{:S(2)}) copy-start(s32[32]{0:T(128)} %param.12) | copy-start | bytes 388
  0.0 106.0 %copy-start.4 = (s32[32]{0:T(128)S(1)}, s32[32]{0:T(128)}, u32[]{:S(2)}) copy-start(s32[32]{0:T(128)} %param.14) | copy-start | bytes 388
  0.0 106.0 %copy-start.2 = (s32[384]{0:T(512)S(1)}, s32[384]{0:T(512)}, u32[]{:S(2)}) copy-start(s32[384]{0:T(512)} %param.13) | copy-start | bytes 4612
  0.0 106.0 %copy-start.1 = (f32[384]{0:T(512)S(1)}, f32[384]{0:T(512)}, u32[]{:S(2)}) copy-start(f32[384]{0:T(512)} %param.11) | copy-start | bytes 4612
  0.0 106.0 %copy-start.3 = (f32[32]{0:T(128)S(1)}, f32[32]{0:T(128)}, u32[]{:S(2)}) copy-start(f32[32]{0:T(128)} %param.10) | copy-start | bytes 388
